TPU v7x, 512 devices: a whole 4x4x16 slice. The times are simulated.
512 devices in a mesh: pair: 128 (over x, z, core), sect: 4 (over y).
Axes of the slice: x: 4, y: 4, z: 16, core: 2. Of those that a mesh axis runs over, the one named last changes fastest.
Arguments:
- operators: float32 [256, 1024, 1024], P('pair', 'sect'), may hold values from -6 to 6
- rotations: float32 [128, 1024, 768], P('pair', 'sect'), may hold values from -0.1875 to 0.1875
- sector_owner: int32 [1], replicated, may hold values from 0 to 127
- slot_pair: int32 [256], replicated, may hold values from 0 to 255, each once
- sources: int32 [256, 16], replicated, may hold values from 0 to 255
- integrals: float32 [256, 16], replicated, may hold values from -3 to 3
- term_count: int32 [256], replicated, may hold values from 1 to 16, 1024 in all
Outputs:
- complement: float32 [256, 768, 768], P('pair', 'sect')
Inputs may be any that keep to these rules, and one draw needn't show every extreme that they name: `sector_owner`: a pair index along the pair axis. `slot_pair`: each orbital-pair id appears once. `sources`: ids may repeat within a list. `term_count`: the counts sum to 1024 and the largest is exactly 16.
All inputs are finite; a program needn't handle non-finite values.
Results may differ from a plain program's by a relative error of at most 0.0001.
Values sent between devices are 32-bit elements; how exact they have to be, the bound alone decides.
No kernel may reach another device: no remote copies, remote signals or barrier semaphores. Data moves between devices by JAX's collectives and lax.ppermute only.
A program may use at most 64 MiB of HBM per device.

v0:
```python
import jax
import jax.numpy as jnp
from jax import lax
from jax.sharding import PartitionSpec as P


def broadcast(value, axis, root):
    mine = lax.axis_index(axis) == root
    return lax.psum(jnp.where(mine, value, jnp.zeros_like(value)), axis)


def coupling_matrix(slot_pair, sources, integrals, term_count):
    is_live = lax.broadcasted_iota(jnp.int32, sources.shape, 1) < term_count[:, None]
    weighted = jnp.where(is_live, integrals, jnp.zeros_like(integrals))
    matches = (sources[:, :, None] == slot_pair[None, None, :]).astype(jnp.float32)
    return jnp.sum(weighted[:, :, None] * matches, axis=1)


def on_device(operators, rotations, sector_owner, slot_pair, sources, integrals, term_count):
    owner_rank = sector_owner[0]
    whole_rows = lax.all_gather(rotations[0], "sect", axis=0, tiled=True)
    rotation_full = broadcast(whole_rows, "pair", owner_rank)
    sect_count = lax.axis_size("sect")
    pair_count = lax.axis_size("pair")
    local_ops = operators.shape[0]
    width_new = rotation_full.shape[1]
    new_rows = width_new // sect_count
    right_done = jnp.einsum(
        "oij,jb->oib",
        operators,
        rotation_full,
        precision=lax.Precision.HIGHEST,
        preferred_element_type=jnp.float32,
    )
    columns = lax.dynamic_slice_in_dim(
        rotation_full, lax.axis_index("sect") * new_rows, new_rows, 1
    )
    rotated = jnp.einsum(
        "ia,oib->oab",
        columns,
        lax.all_gather(right_done, "sect", axis=1, tiled=True),
        precision=lax.Precision.HIGHEST,
        preferred_element_type=jnp.float32,
    )
    coupling = coupling_matrix(slot_pair, sources, integrals, term_count)
    blocks = rotated.reshape(local_ops, pair_count, -1)
    mixture = jnp.einsum(
        "or,rhn->ohn",
        coupling,
        lax.all_to_all(blocks, "pair", split_axis=1, concat_axis=0, tiled=True),
        precision=lax.Precision.HIGHEST,
        preferred_element_type=jnp.float32,
    )
    result = lax.all_to_all(mixture, "pair", split_axis=0, concat_axis=1, tiled=True)
    return result.reshape(local_ops, new_rows, width_new)


def solution(mesh):
    in_specs = (P("pair", "sect", None), P("pair", "sect", None), P(), P(), P(), P(), P())
    out_specs = P("pair", "sect", None)
    return jax.shard_map(
        on_device, mesh=mesh, in_specs=in_specs, out_specs=out_specs, check_vma=False
    )
```

profile of v0, /device:TPU:2, one launch (start us, length us, event | category | flops | bytes accessed | tf_op | source)
XLA Modules:
  0.0 676.5 jit_solution(10659729526781779810)
XLA Ops:
  6.5 0.0 copy-start
  6.5 0.0 all-gather.6.cloned.1.call-start
  6.5 2.4 copy.26
  9.0 0.0 all-gather.6.cloned.1.call-update
  9.0 0.0 all-reduce.2.cloned.1.call-start
  9.7 51.4 %all-gather.6.cloned.1.call-done = f32[1,1024,768]{1,2,0:T(8,128)} async-done(((f32[1,256,768]{1,2,0:T(8,128)}), f32[1,1024,768]{1,2,0:T(8,128)}) %all-gather.6.cloned.1.call-update) | async-done | bytes 3145744 | tf_op jit(solution)/shard_map/all_gather | solution.py:21
  61.1 2.2 select_bitcast_fusion
  63.3 0.0 all-reduce.2.cloned.1.call-update
  63.4 0.0 all-gather.4.cloned.1.call-start
  63.4 359.1 %all-reduce.2.cloned.1.call-done = f32[1024,768]{0,1:T(8,128)} async-done(((f32[1024,768]{0,1:T(8,128)}), f32[1024,768]{0,1:T(8,128)}) %all-reduce.2.cloned.1.call-update) | async-done | bytes 3145744 | tf_op jit(solution)/shard_map/psum | solution.py:9
  422.5 0.0 copy-done
  422.5 8.1 %fusion.2 = f32[2,256,768]{1,2,0:T(8,128)} fusion(f32[2,256,1024]{2,1,0:T(8,128)S(1)} %copy-done, f32[1024,768]{0,1:T(8,128)} %all-reduce.2.cloned.1.call-done), kind=kOutput, calls=%fused_computation.5 | convolution fusion | flops 4831838208 | bytes 6815744 | tf_op jit(solution)/shard_map/oij,jb->oib/dot_general | solution.py:28
  430.6 0.0 all-gather.4.cloned.1.call-update
  430.6 71.9 %all-gather.4.cloned.1.call-done = f32[2,1024,768]{1,2,0:T(8,128)} async-done(((f32[2,256,768]{1,2,0:T(8,128)}), f32[2,1024,768]{1,2,0:T(8,128)}) %all-gather.4.cloned.1.call-update) | async-done | bytes 6291472 | tf_op jit(solution)/shard_map/all_gather | solution.py:41
  502.5 10.6 %convolution_bitcast_fusion.1 = f32[2,192,768]{2,1,0:T(8,128)} fusion(f32[2,1024,768]{1,2,0:T(8,128)} %all-gather.4.cloned.1.call-done, f32[1024,768]{0,1:T(8,128)} %all-reduce.2.cloned.1.call-done, s32[]{:T(128)S(6)} %select_n.18), kind=kOutput, calls=%fused_computation.6 | convolution fusion | flops 3623878656 | bytes 8257540 | tf_op jit(solution)/shard_map/ia,oib->oab/dot_general | solution.py:38
  513.1 1.6 reshape.16
  514.7 0.0 copy-start.2
  514.7 0.0 copy-start.4
  514.7 0.0 copy-start.1
  514.7 0.0 copy-start.3
  514.7 1.9 copy.28
  516.6 16.6 %all-to-all-start = ((f32[2,128,1152]{2,0,1:T(2,128)}), f32[2,128,1152]{2,0,1:T(2,128)S(1)}, u32[]{:S(2)}, u32[]{:S(2)}) async-start(f32[2,128,1152]{2,0,1:T(2,128)} %copy.28), calls=%async_computation | async-start | bytes 2359296 | tf_op jit(solution)/shard_map/all_to_all | solution.py:50
  533.2 0.0 copy-done.2
  533.2 0.0 copy-done.4
  533.3 0.7 copy.25
  534.0 0.0 copy-done.1
  534.0 0.8 copy.24
  534.8 0.0 copy-done.3
  534.8 2.8 select_reduce_fusion
  537.5 57.2 %all-to-all-done = f32[2,128,1152]{2,0,1:T(2,128)S(1)} async-done(((f32[2,128,1152]{2,0,1:T(2,128)}), f32[2,128,1152]{2,0,1:T(2,128)S(1)}, u32[]{:S(2)}, u32[]{:S(2)}) %all-to-all-start) | async-done | bytes 1179680 | tf_op jit(solution)/shard_map/all_to_all | solution.py:50
  594.7 1.8 reshape.17
  596.6 2.5 convolution_bitcast_fusion
  599.1 1.2 copy.29
  600.3 68.2 %all_to_all.30 = f32[256,1,1152]{2,1,0:T(1,128)S(1)} all-to-all(f32[256,1,1152]{2,1,0:T(1,128)S(1)} %copy.29), channel_id=1, replica_groups=mesh['pair'=128,'sect'=4] {'pair'}, dimensions={0} | all-to-all | bytes 2359296 | tf_op jit(solution)/shard_map/all_to_all | solution.py:54
  668.5 0.1 copy.30
  668.6 1.3 reshape.18
  (1 shorter events, 0.0 us)
Async XLA Ops:
  6.5 416.0 %copy-start = (f32[2,256,1024]{2,1,0:T(8,128)S(1)}, f32[2,256,1024]{2,1,0:T(8,128)}, u32[]{:S(2)}) copy-start(f32[2,256,1024]{2,1,0:T(8,128)} %param.7) | copy-start | bytes 6291460
  6.5 54.6 %all-gather.6.cloned.1.call-start = ((), (), s32[]{:S(2)}) async-start(), calls=%async_computation.4 | async-start | bytes 3932160 | tf_op jit(solution)/shard_map/all_gather | solution.py:21
  9.0 413.5 %all-reduce.2.cloned.1.call-start = ((), (), s32[]{:S(2)}) async-start(), calls=%async_computation.2 | async-start | bytes 6291456 | tf_op jit(solution)/shard_map/psum | solution.py:9
  63.4 439.1 %all-gather.4.cloned.1.call-start = ((), (), s32[]{:S(2)}) async-start(), calls=%async_computation.3 | async-start | bytes 7864320 | tf_op jit(solution)/shard_map/all_gather | solution.py:41
  514.7 18.6 %copy-start.2 = (f32[256,16]{0,1:T(8,128)S(1)}, f32[256,16]{0,1:T(8,128)}, u32[]{:S(2)}) copy-start(f32[256,16]{0,1:T(8,128)} %param.12) | copy-start | bytes 49156
  514.7 18.6 %copy-start.4 = (s32[256]{0:T(256)S(1)}, s32[256]{0:T(256)}, u32[]{:S(2)}) copy-start(s32[256]{0:T(256)} %param.13) | copy-start | bytes 3076
  514.7 19.3 %copy-start.1 = (s32[256,16]{0,1:T(8,128)S(1)}, s32[256,16]{0,1:T(8,128)}, u32[]{:S(2)}) copy-start(s32[256,16]{0,1:T(8,128)} %param.11) | copy-start | bytes 49156
  514.7 20.1 %copy-start.3 = (s32[256]{0:T(256)S(1)}, s32[256]{0:T(256)}, u32[]{:S(2)}) copy-start(s32[256]{0:T(256)} %param.10) | copy-start | bytes 3076
  516.6 78.1 %all-to-all-start = ((f32[2,128,1152]{2,0,1:T(2,128)}), f32[2,128,1152]{2,0,1:T(2,128)S(1)}, u32[]{:S(2)}, u32[]{:S(2)}) async-start(f32[2,128,1152]{2,0,1:T(2,128)} %copy.28), calls=%async_computation | async-start | bytes 2359296 | tf_op jit(solution)/shard_map/all_to_all | solution.py:50
Sparse Core Ops, SparseCore 0:
  9.4 51.6 all-gather.5
  64.6 357.9 all-reduce.1
  430.8 71.7 all-gather.3
where the time goes:
time: 677 us; the launch traced here: 676 us
  waiting for transfers between devices  540 us (80%)
  blocking collectives  68.2 us (10%)
  matrix products  21.1 us (3%)
  starting transfers between devices  16.7 us (2%)
  between operations  13.9 us (2%)
  local copies, waits for them, and re-layouts  11.9 us (2%)
    psum x1, waiting for transfers between devices, broadcast(): return lax.psum(jnp.where(mine, value, jnp.zeros_like(value)), axis)  359 us
    all_gather x1, waiting for transfers between devices, on_device(): lax.all_gather(right_done, 'sect', axis=1, tiled=True)  71.9 us
    all_to_all x1, blocking collectives, on_device(): lax.all_to_all(mixture, 'pair', split_axis=0, concat_axis=1, tiled=True)  68.2 us
    all_to_all x1, waiting for transfers between devices, on_device(): lax.all_to_all(blocks, 'pair', split_axis=1, concat_axis=0, tiled=True)  57.2 us
    all_gather x1, waiting for transfers between devices, on_device(): whole_rows = lax.all_gather(rotations[0], 'sect', axis=0, tiled=True)  51.4 us
    all_to_all x1, starting transfers between devices, on_device(): lax.all_to_all(blocks, 'pair', split_axis=1, concat_axis=0, tiled=True)  16.6 us
  transfers between devices with their start and end apart: 4, of which 4 were waited for; matrix products, arithmetic and copies ran while one was open for 1% of the time, Pallas kernels for 0%

commit v1 on v0

v1 whole, which is shorter than its diff:
```python
import jax
import jax.numpy as jnp
from jax import lax
from jax.experimental import pallas as pl
from jax.experimental.pallas import tpu as pltpu
from jax.sharding import Mesh, PartitionSpec as P


NX, NZ, NC, NY = 4, 16, 2, 4
N_PAIR = NX * NZ * NC
PAIR = ("x", "z", "c")
LANES = 128
F32, BF16 = jnp.float32, jnp.bfloat16


def exchange(chunks, axes):
    return lax.all_to_all(chunks, axes, split_axis=0, concat_axis=0, tiled=True)


def gather(piece, axes, count):
    return exchange(jnp.broadcast_to(piece, (count, *piece.shape)), axes)


def two_parts(value):
    high = value.astype(BF16)
    return high, (value - high.astype(F32)).astype(BF16)


def dot3(left, right, dims):
    (lh, ll), (rh, rl) = left, right

    def one(a, b):
        return lax.dot_general(a, b, (dims, ((), ())), preferred_element_type=F32)

    return one(lh, rh) + (one(lh, rl) + one(ll, rh))


def spread_rotation(slab, owner):
    x_own, z_own, c_own = owner // (NZ * NC), (owner // NC) % NZ, owner % NC
    flipped = slab.T
    new, few = flipped.shape
    rows = new // (NC * NX)
    piece = exchange(flipped.reshape(NC * NX, rows, few), ("c", "x"))
    piece = lax.dynamic_index_in_dim(piece, c_own * NX + x_own, 0, keepdims=False)
    piece = exchange(piece.reshape(NZ, rows // NZ, few), "z")
    piece = lax.dynamic_index_in_dim(piece, z_own, 0, keepdims=False)
    piece = gather(piece, "z", NZ).reshape(rows, few)
    piece = gather(piece, ("y", "x"), NY * NX)
    return piece.reshape(NY, NX * rows, few)


def split_columns(operators, y):
    n_ops, few, old = operators.shape
    cols = old // NY

    def body(y_ref, *refs):
        for source, target in zip(refs[:NY], refs[NY:], strict=True):
            target[...] = source[0]

    return pl.pallas_call(
        body,
        grid_spec=pltpu.PrefetchScalarGridSpec(
            num_scalar_prefetch=1,
            grid=(n_ops,),
            in_specs=[
                pl.BlockSpec((1, few, cols), lambda g, y_ref, hop=hop: (g, 0, lax.rem(y_ref[0] + hop, NY)))
                for hop in range(NY)
            ],
            out_specs=[pl.BlockSpec((few, cols), lambda g, y_ref: (0, g))] * NY,
        ),
        out_shape=[jax.ShapeDtypeStruct((few, n_ops * cols), F32)] * NY,
        cost_estimate=pl.CostEstimate(flops=0, bytes_accessed=8 * operators.size, transcendentals=0),
        name="split_columns",
    )(y, *[operators] * NY)


def multiply_left(place, half, blocks, before=None):
    n_half, few = half.shape[1:]
    wide = blocks[0].shape[1]
    rows = NY * n_half // 2 // NY

    def body(place_ref, half_ref, *refs):
        block_refs, refs = refs[:NY], refs[NY:]
        out_ref, th, tl, oh, ol = refs[-5:]
        for hop in range(NY):
            part = pl.ds(hop * few, few)
            th[:, part], tl[:, part] = two_parts(half_ref[lax.rem(place_ref[0] + NY - hop, NY)])
            oh[part, :], ol[part, :] = two_parts(block_refs[hop][...])
        done = dot3((th[...], tl[...]), (oh[...], ol[...]), ((1,), (0,)))
        for q in range(2):
            out_ref[q] = done[q * rows : (q + 1) * rows]

    whole = lambda *shape: pl.BlockSpec(shape, lambda i, place_ref: (0,) * len(shape))
    extra = [] if before is None else [before]
    return pl.pallas_call(
        body,
        grid_spec=pltpu.PrefetchScalarGridSpec(
            num_scalar_prefetch=1,
            grid=(1,),
            in_specs=[whole(*half.shape)]
            + [whole(*b.shape) for b in blocks]
            + [pl.BlockSpec(memory_space=pl.ANY)] * len(extra),
            out_specs=pl.BlockSpec((2, rows, wide), lambda i, place_ref: (place_ref[1], 0, 0)),
            scratch_shapes=[
                pltpu.VMEM((n_half, NY * few), BF16),
                pltpu.VMEM((n_half, NY * few), BF16),
                pltpu.VMEM((NY * few, wide), BF16),
                pltpu.VMEM((NY * few, wide), BF16),
            ],
        ),
        out_shape=jax.ShapeDtypeStruct((4, rows, wide), F32),
        input_output_aliases={} if before is None else {2 + NY: 0},
        cost_estimate=pl.CostEstimate(
            flops=6 * n_half * NY * few * wide, bytes_accessed=4 * half.size + 20 * blocks[0].size, transcendentals=0
        ),
        name="multiply_left",
    )(place, half, *blocks, *extra)


def multiply_right(core, by_row, own, other):
    rows = by_row.shape[1]
    n_half, few = own.shape[1:]
    n_ops = by_row.shape[2] // few
    triples, strips = rows // 3, n_half // LANES
    per = n_ops * 3 * strips

    def body(core_ref, row_ref, own_ref, other_ref, out_ref, rh, rl, th, tl, z):
        for s in range(NY):
            part = pl.ds(s * few, few)
            for g in range(n_ops):
                band = pl.ds(g * rows, rows)
                rh[band, part], rl[band, part] = two_parts(row_ref[s, :, g * few : (g + 1) * few])
        for turn, ref in enumerate((own_ref, other_ref)):
            for s in range(NY):
                part = pl.ds(s * few, few)
                th[:, part], tl[:, part] = two_parts(ref[s])
            done = dot3((rh[...], rl[...]), (th[...], tl[...]), ((1,), (1,)))
            side = core_ref[0] if turn == 0 else 1 - core_ref[0]
            for strip in range(strips):
                z[strip] = done[:, strip * LANES : (strip + 1) * LANES]
            for g in range(n_ops):
                for r in range(3):
                    for strip in range(strips):
                        at = g * 3 * strips + r * strips + strip
                        out_ref[side, pl.ds(at, triples, stride=per), :] = z[
                            strip, pl.ds(g * rows + r, triples, stride=3), :
                        ]

    whole = lambda *shape: pl.BlockSpec(shape, lambda i, core_ref: (0,) * len(shape))
    out = (2, triples * per, LANES)
    return pl.pallas_call(
        body,
        grid_spec=pltpu.PrefetchScalarGridSpec(
            num_scalar_prefetch=1,
            grid=(1,),
            in_specs=[whole(*by_row.shape), whole(*own.shape), whole(*other.shape)],
            out_specs=whole(*out),
            scratch_shapes=[
                pltpu.VMEM((n_ops * rows, NY * few), BF16),
                pltpu.VMEM((n_ops * rows, NY * few), BF16),
                pltpu.VMEM((n_half, NY * few), BF16),
                pltpu.VMEM((n_half, NY * few), BF16),
                pltpu.VMEM((strips, n_ops * rows, LANES), F32),
            ],
        ),
        out_shape=jax.ShapeDtypeStruct(out, F32),
        cost_estimate=pl.CostEstimate(
            flops=12 * n_ops * rows * NY * few * n_half, bytes_accessed=16 * own.size, transcendentals=0
        ),
        name="multiply_right",
    )(core, by_row, own, other)


def mix(coupling, spread):
    n_all = coupling.shape[0]
    n_ops = n_all // N_PAIR
    per = spread.shape[0] // N_PAIR
    strips = per // n_ops

    def body(c_ref, x_ref, out_ref, xh, xl):
        for g in range(n_ops):
            for k in range(strips):
                part = x_ref[pl.ds(g * strips + k, N_PAIR, stride=per), :]
                at = (pl.ds(g * N_PAIR, N_PAIR), pl.ds(k * LANES, LANES))
                xh[at], xl[at] = two_parts(part)
        done = dot3(two_parts(c_ref[...]), (xh[...], xl[...]), ((1,), (0,)))
        for g in range(n_ops):
            for k in range(strips):
                out_ref[pl.ds(g * strips + k, N_PAIR, stride=per), :] = done[
                    g * N_PAIR : (g + 1) * N_PAIR, k * LANES : (k + 1) * LANES
                ]

    return pl.pallas_call(
        body,
        out_shape=jax.ShapeDtypeStruct(spread.shape, F32),
        scratch_shapes=[pltpu.VMEM((n_all, strips * LANES), BF16)] * 2,
        cost_estimate=pl.CostEstimate(
            flops=6 * n_all * n_all * strips * LANES, bytes_accessed=8 * spread.size, transcendentals=0
        ),
        name="mix",
    )(coupling, spread)


def place_rows(back, rows, width):
    triples = rows // 3
    strips = width // 2 // LANES
    per = back.shape[0] // (2 * triples)
    n_ops = per // (3 * strips)

    def body(in_ref, out_ref, band):
        for g in range(n_ops):
            for h in range(2):
                for strip in range(strips):
                    for r in range(3):
                        at = h * triples * per + g * 3 * strips + r * strips + strip
                        band[g, h, strip, pl.ds(r, triples, stride=3), :] = in_ref[pl.ds(at, triples, stride=per), :]
                    lanes = pl.ds((h * strips + strip) * LANES, LANES)
                    out_ref[g, :, lanes] = band[g, h, strip]

    return pl.pallas_call(
        body,
        out_shape=jax.ShapeDtypeStruct((n_ops, rows, width), F32),
        scratch_shapes=[pltpu.VMEM((n_ops, 2, strips, rows, LANES), F32)],
        cost_estimate=pl.CostEstimate(flops=0, bytes_accessed=8 * back.size, transcendentals=0),
        name="place_rows",
    )(back)


def coupling_matrix(slot_pair, sources, integrals, term_count):
    is_live = lax.broadcasted_iota(jnp.int32, sources.shape, 1) < term_count[:, None]
    weighted = jnp.where(is_live, integrals, jnp.zeros_like(integrals))
    matches = (sources[:, :, None] == slot_pair[None, None, :]).astype(F32)
    return jnp.sum(weighted[:, :, None] * matches, axis=1)


def by_slot(values, n_ops):
    rest = values.shape[1:]
    values = values.reshape(NX * NZ, NC, n_ops, *rest)
    return jnp.moveaxis(values, (2, 1, 0), (0, 1, 2)).reshape(-1, *rest)


def on_device(operators, rotations, sector_owner, slot_pair, sources, integrals, term_count):
    n_ops, _, _ = operators.shape
    y, c = lax.axis_index("y"), lax.axis_index("c")
    blocks = list(split_columns(operators, y[None]))
    for hop in range(1, NY):
        blocks[hop] = lax.ppermute(blocks[hop], "y", [(i, (i + hop) % NY) for i in range(NY)])
    coupling = coupling_matrix(*[by_slot(v, n_ops) for v in (slot_pair, sources, integrals, term_count)])
    own = spread_rotation(rotations[0], sector_owner[0])
    other = lax.ppermute(own, "c", [(0, 1), (1, 0)])
    width = rotations.shape[2]
    rows = width // NY
    left_done = multiply_left(jnp.stack([y, c]), own, blocks)
    left_done = multiply_left(jnp.stack([y, 1 - c]), other, blocks, left_done)
    by_row = exchange(left_done, "y")
    chunks = multiply_right(c[None], by_row, own, other)
    spread = exchange(chunks.reshape(N_PAIR, -1), ("c", "x", "z"))
    mixture = mix(coupling, spread.reshape(-1, LANES))
    back = exchange(mixture.reshape(N_PAIR, -1), ("c", "x", "z"))
    return place_rows(back.reshape(-1, LANES), rows, width)


def solution(mesh):
    torus = Mesh(mesh.devices.reshape(NX, NZ, NC, NY), ("x", "z", "c", "y"))

    in_specs = (P(PAIR, "y", None), P(PAIR, "y", None), P(), P(), P(), P(), P())
    return jax.shard_map(on_device, mesh=torus, in_specs=in_specs, out_specs=P(PAIR, "y", None), check_vma=False)
```

time: 677 us -> 315 us (0.47)
  the two profiles are of different devices: /device:TPU:2 before, /device:TPU:34 now
where the time goes in v1:
time: 315 us; the launch traced here: 314 us
  blocking collectives  137 us (43%)
  waiting for transfers between devices  103 us (33%)
  starting transfers between devices  39.9 us (13%)
  Pallas kernels  24.3 us (8%)
  local copies, waits for them, and re-layouts  6.15 us (2%)
    all_to_all x4, blocking collectives, exchange(): return lax.all_to_all(chunks, axes, split_axis=0, concat_axis=0, tiled=True)  137 us
    all_to_all x3, waiting for transfers between devices, exchange(): return lax.all_to_all(chunks, axes, split_axis=0, concat_axis=0, tiled=True)  81.7 us
    all_to_all x3, starting transfers between devices, exchange(): return lax.all_to_all(chunks, axes, split_axis=0, concat_axis=0, tiled=True)  28.7 us
    ppermute x3, waiting for transfers between devices, on_device(): lax.ppermute(blocks[hop], 'y', [(i, (i + hop) % NY) for i in range(NY)])  21.5 us
    pallas_call x2, Pallas kernels, multiply_left(): pl.pallas_call(body, grid_spec=pltpu.PrefetchScalarGridSpec(num_scalar_pr...  9.86 us
    ppermute x3, starting transfers between devices, on_device(): lax.ppermute(blocks[hop], 'y', [(i, (i + hop) % NY) for i in range(NY)])  9.21 us
  transfers between devices with their start and end apart: 7, of which 5 were waited for; matrix products, arithmetic and copies ran while one was open for 1% of the time, Pallas kernels for 2%

profile of v1, /device:TPU:34, one launch (start us, length us, event | category | flops | bytes accessed | tf_op | source)
XLA Modules:
  0.0 314.4 jit_solution(13124564030448637758)
XLA Ops:
  0.0 2.3 copy.37
  2.3 4.8 %all-to-all-start = ((f32[8,96,256]{2,1,0:T(8,128)}), f32[8,96,256]{2,1,0:T(8,128)S(1)}, u32[]{:S(2)}, u32[]{:S(2)}) async-start(f32[8,96,256]{2,1,0:T(8,128)} %bitcast.12), calls=%async_computation | async-start | bytes 1572864 | tf_op jit(solution)/shard_map/all_to_all | solution.py:17
  7.8 10.4 %all-to-all-done = f32[8,96,256]{2,1,0:T(8,128)S(1)} async-done(((f32[8,96,256]{2,1,0:T(8,128)}), f32[8,96,256]{2,1,0:T(8,128)S(1)}, u32[]{:S(2)}, u32[]{:S(2)}) %all-to-all-start) | async-done | bytes 786464 | tf_op jit(solution)/shard_map/all_to_all | solution.py:17
  18.2 0.7 reshape.79
  18.9 15.2 %all-to-all-start.1 = ((f32[16,6,256]{2,1,0:T(8,128)}), f32[16,6,256]{2,1,0:T(8,128)S(1)}, u32[]{:S(2)}, u32[]{:S(2)}) async-start(f32[16,6,256]{2,1,0:T(8,128)} %reshape.79), calls=%async_computation.1 | async-start | bytes 262144 | tf_op jit(solution)/shard_map/all_to_all | solution.py:17
  34.1 14.4 %all-to-all-done.1 = f32[16,6,256]{2,1,0:T(8,128)S(1)} async-done(((f32[16,6,256]{2,1,0:T(8,128)}), f32[16,6,256]{2,1,0:T(8,128)S(1)}, u32[]{:S(2)}, u32[]{:S(2)}) %all-to-all-start.1) | async-done | bytes 98336 | tf_op jit(solution)/shard_map/all_to_all | solution.py:17
  48.5 18.9 %all_to_all.43 = f32[16,6,256]{2,1,0:T(8,128)S(1)} all-to-all(f32[16,6,256]{2,1,0:T(8,128)S(1)} %broadcast_in_dim.16), channel_id=1, replica_groups=mesh['x'=4,'z'=16,'c'=2,'y'=4] {'z'}, dimensions={0} | all-to-all | bytes 196608 | tf_op jit(solution)/shard_map/all_to_all | solution.py:17
  67.5 0.1 broadcast_in_dim.17
  67.6 24.7 %all_to_all.44 = f32[16,96,256]{2,1,0:T(8,128)S(1)} all-to-all(f32[16,96,256]{2,1,0:T(8,128)S(1)} %broadcast_in_dim.17), channel_id=1, replica_groups=mesh['x'=4,'z'=16,'c'=2,'y'=4] {'y','x'}, dimensions={0} | all-to-all | bytes 3145728 | tf_op jit(solution)/shard_map/all_to_all | solution.py:17
  92.3 1.9 collective-permute-start
  94.2 2.6 split_columns.1
  96.9 0.0 copy-done
  96.9 1.9 collective-permute-start.1
  98.8 4.2 %collective-permute-start.2 = (f32[256,512]{1,0:T(8,128)}, f32[256,512]{1,0:T(8,128)S(1)}, u32[]{:S(2)}, u32[]{:S(2)}) collective-permute-start(f32[256,512]{1,0:T(8,128)} %get-tuple-element.11), channel_id=1, source_target_pairs={{0,2},{1,3},{2,0},{3,1},{4,6},{5,7},{6,4},{7,5},{8,10},{9,11},{10,... | collective-permute-start | bytes 1572872 | tf_op jit(solution)/shard_map/ppermute | solution.py:247
  103.0 3.1 collective-permute-start.3
  106.1 0.6 pad_add_fusion
  106.7 19.0 %collective-permute-done.1.refs_1_ = f32[256,512]{1,0:T(8,128)S(1)} collective-permute-done((f32[256,512]{1,0:T(8,128)}, f32[256,512]{1,0:T(8,128)S(1)}, u32[]{:S(2)}, u32[]{:S(2)}) %collective-permute-start.1) | collective-permute-done | bytes 524320 | tf_op jit(solution)/shard_map/ppermute | solution.py:247
  125.7 0.0 collective-permute-done.2.refs_2_
  125.8 2.5 collective-permute-done.3.refs_3_
  128.3 0.0 copy-done.2
  128.3 0.0 copy-done.3
  128.3 0.8 copy-done.4
  129.1 4.9 %multiply_left.2.refs_4_ = f32[4,192,512]{2,1,0:T(8,128)} custom-call(s32[2]{0:T(128)} %get-tuple-element.14.place_ref, f32[4,384,256]{2,1,0:T(8,128)} %bitcast.32, f32[256,512]{1,0:T(8,128)} %get-tuple-element.9.refs_0_, f32[256,512]{1,0:T(8,128)} %copy-done.2, f32[256,512]{1,0:T(8,128)} %copy-done.3, f32[256,512]{1,0:T(8,128)} %copy-done.4), custom_call_target="tpu_custom_call" | custom-call | flops 1207959552 | bytes 4194304 | tf_op jit(solution)/shard_map/multiply_left/pallas_call | solution.py:95
  134.0 0.0 collective-permute-done.half_ref.other_ref
  134.0 4.9 %multiply_left.3 = f32[4,192,512]{2,1,0:T(8,128)} custom-call(s32[2]{0:T(128)} %get-tuple-element.13.place_ref, f32[4,384,256]{2,1,0:T(8,128)} %collective-permute-done.half_ref.other_ref, f32[256,512]{1,0:T(8,128)} %get-tuple-element.9.refs_0_, f32[256,512]{1,0:T(8,128)} %copy-done.2, f32[256,512]{1,0:T(8,128)} %copy-done.3, ...), custom_call_target="tpu_custom_call", output_to_operand_aliasing={{}: (6, {})} | custom-call | flops 1207959552 | bytes 4194304 | tf_op jit(solution)/shard_map/multiply_left/pallas_call | solution.py:95
  139.0 25.0 %all_to_all.45.row_ref = f32[4,192,512]{2,1,0:T(8,128)} all-to-all(f32[4,192,512]{2,1,0:T(8,128)} %multiply_left.3), channel_id=1, replica_groups=mesh['x'=4,'z'=16,'c'=2,'y'=4] {'y'}, dimensions={0} | all-to-all | bytes 3145728 | tf_op jit(solution)/shard_map/all_to_all | solution.py:17
  163.9 6.1 %multiply_right.1 = f32[2,1152,128]{2,1,0:T(8,128)} custom-call(s32[1]{0:T(128)} %bitcast.7.core_ref, f32[4,192,512]{2,1,0:T(8,128)} %all_to_all.45.row_ref, f32[4,384,256]{2,1,0:T(8,128)} %bitcast.33, f32[4,384,256]{2,1,0:T(8,128)} %collective-permute-done.half_ref.other_ref), custom_call_target="tpu_custom_call" | custom-call | flops 1811939328 | bytes 6291456 | tf_op jit(solution)/shard_map/multiply_right/pallas_call | solution.py:151
  170.0 8.7 %all-to-all-start.5 = ((f32[128,1,2304]{2,1,0:T(1,128)}), f32[128,1,2304]{2,1,0:T(1,128)S(1)}, u32[]{:S(2)}, u32[]{:S(2)}) async-start(f32[128,1,2304]{2,1,0:T(1,128)} %bitcast.37), calls=%async_computation.5 | async-start | bytes 2359296 | tf_op jit(solution)/shard_map/all_to_all | solution.py:17
  178.7 0.0 copy-done.5
  178.7 0.1 copy.34
  178.8 0.1 copy.35
  178.9 0.1 reshape.77
  179.0 0.0 copy-done.7
  179.0 0.2 reshape.75
  179.2 0.1 copy.33
  179.3 0.1 lt.32
  179.4 0.1 copy.36
  179.5 0.0 copy-done.6
  179.5 0.1 copy.29
  179.6 0.2 reshape.74
  179.8 0.1 copy.32
  179.9 0.1 eq.22
  180.0 2.3 select_reduce_fusion.c_ref
  182.3 56.9 %all-to-all-done.5 = f32[128,1,2304]{2,1,0:T(1,128)S(1)} async-done(((f32[128,1,2304]{2,1,0:T(1,128)}), f32[128,1,2304]{2,1,0:T(1,128)S(1)}, u32[]{:S(2)}, u32[]{:S(2)}) %all-to-all-start.5) | async-done | bytes 1179680 | tf_op jit(solution)/shard_map/all_to_all | solution.py:17
  239.2 1.0 copy-done.1
  240.2 3.2 %mix.1 = f32[2304,128]{1,0:T(8,128)} custom-call(f32[256,256]{1,0:T(8,128)} %select_reduce_fusion.c_ref, f32[2304,128]{1,0:T(8,128)} %bitcast.34), custom_call_target="tpu_custom_call" | custom-call | flops 452984832 | bytes 2359296 | tf_op jit(solution)/shard_map/mix/pallas_call | solution.py:193
  243.4 68.5 %all_to_all.46 = f32[128,1,2304]{2,1,0:T(1,128)} all-to-all(f32[128,1,2304]{2,1,0:T(1,128)} %bitcast.35), channel_id=1, replica_groups=mesh['x'=4,'z'=16,'c'=2,'y'=4] {'c','x','z'}, dimensions={0} | all-to-all | bytes 2359296 | tf_op jit(solution)/shard_map/all_to_all | solution.py:17
  312.0 2.5 place_rows.1
  (16 shorter events, 0.1 us)
Async XLA Ops:
  2.3 15.9 %all-to-all-start = ((f32[8,96,256]{2,1,0:T(8,128)}), f32[8,96,256]{2,1,0:T(8,128)S(1)}, u32[]{:S(2)}, u32[]{:S(2)}) async-start(f32[8,96,256]{2,1,0:T(8,128)} %bitcast.12), calls=%async_computation | async-start | bytes 1572864 | tf_op jit(solution)/shard_map/all_to_all | solution.py:17
  18.9 29.6 %all-to-all-start.1 = ((f32[16,6,256]{2,1,0:T(8,128)}), f32[16,6,256]{2,1,0:T(8,128)S(1)}, u32[]{:S(2)}, u32[]{:S(2)}) async-start(f32[16,6,256]{2,1,0:T(8,128)} %reshape.79), calls=%async_computation.1 | async-start | bytes 262144 | tf_op jit(solution)/shard_map/all_to_all | solution.py:17
  92.3 4.6 %copy-start = (f32[16,96,256]{2,1,0:T(8,128)}, f32[16,96,256]{2,1,0:T(8,128)S(1)}, u32[]{:S(2)}) copy-start(f32[16,96,256]{2,1,0:T(8,128)S(1)} %all_to_all.44) | copy-start | bytes 4718596
  92.3 41.7 %collective-permute-start = (f32[4,384,256]{2,1,0:T(8,128)S(1)}, f32[4,384,256]{2,1,0:T(8,128)}, u32[]{:S(2)}, u32[]{:S(2)}) collective-permute-start(f32[4,384,256]{2,1,0:T(8,128)S(1)} %bitcast.31), channel_id=1, source_target_pairs={{0,4},{4,0},{1,5},{5,1},{2,6},{6,2},{3,7},{7,3},{8,12},{12,8},{9,1... | collective-permute-start | bytes 4718600 | tf_op jit(solution)/shard_map/ppermute | solution.py:250
  96.9 28.9 %collective-permute-start.1 = (f32[256,512]{1,0:T(8,128)}, f32[256,512]{1,0:T(8,128)S(1)}, u32[]{:S(2)}, u32[]{:S(2)}) collective-permute-start(f32[256,512]{1,0:T(8,128)} %get-tuple-element.10), channel_id=1, source_target_pairs={{0,1},{1,2},{2,3},{3,0},{4,5},{5,6},{6,7},{7,4},{8,9},{9,10},{10,1... | collective-permute-start | bytes 1572872 | tf_op jit(solution)/shard_map/ppermute | solution.py:247
  98.8 27.0 %collective-permute-start.2 = (f32[256,512]{1,0:T(8,128)}, f32[256,512]{1,0:T(8,128)S(1)}, u32[]{:S(2)}, u32[]{:S(2)}) collective-permute-start(f32[256,512]{1,0:T(8,128)} %get-tuple-element.11), channel_id=1, source_target_pairs={{0,2},{1,3},{2,0},{3,1},{4,6},{5,7},{6,4},{7,5},{8,10},{9,11},{10,... | collective-permute-start | bytes 1572872 | tf_op jit(solution)/shard_map/ppermute | solution.py:247
  103.0 25.3 %collective-permute-start.3 = (f32[256,512]{1,0:T(8,128)}, f32[256,512]{1,0:T(8,128)S(1)}, u32[]{:S(2)}, u32[]{:S(2)}) collective-permute-start(f32[256,512]{1,0:T(8,128)} %get-tuple-element.12), channel_id=1, source_target_pairs={{0,3},{1,0},{2,1},{3,2},{4,7},{5,4},{6,5},{7,6},{8,11},{9,8},{10,9... | collective-permute-start | bytes 1572872 | tf_op jit(solution)/shard_map/ppermute | solution.py:247
  125.7 2.5 copy-start.2
  125.8 2.5 copy-start.3
  128.3 0.8 copy-start.4
  170.0 8.7 %copy-start.5 = (f32[256,16]{0,1:T(8,128)S(1)}, f32[256,16]{0,1:T(8,128)}, u32[]{:S(2)}) copy-start(f32[256,16]{0,1:T(8,128)} %param.12) | copy-start | bytes 49156
  170.0 9.0 %copy-start.7 = (s32[256]{0:T(256)S(1)}, s32[256]{0:T(256)}, u32[]{:S(2)}) copy-start(s32[256]{0:T(256)} %param.13) | copy-start | bytes 3076
  170.0 9.5 %copy-start.6 = (s32[256,16]{0,1:T(8,128)S(1)}, s32[256,16]{0,1:T(8,128)}, u32[]{:S(2)}) copy-start(s32[256,16]{0,1:T(8,128)} %param.11) | copy-start | bytes 49156
  170.0 9.6 %copy-start.8 = (s32[256]{0:T(256)S(1)}, s32[256]{0:T(256)}, u32[]{:S(2)}) copy-start(s32[256]{0:T(256)} %param.10) | copy-start | bytes 3076
  170.0 69.2 %all-to-all-start.5 = ((f32[128,1,2304]{2,1,0:T(1,128)}), f32[128,1,2304]{2,1,0:T(1,128)S(1)}, u32[]{:S(2)}, u32[]{:S(2)}) async-start(f32[128,1,2304]{2,1,0:T(1,128)} %bitcast.37), calls=%async_computation.5 | async-start | bytes 2359296 | tf_op jit(solution)/shard_map/all_to_all | solution.py:17
  239.2 1.0 copy-start.1
